TPU v7x, 512 devices: a whole 4x4x16 slice. The times are simulated.
512 devices in a mesh: row: 16 (over z_lo, y), mode: 32 (over z_hi, x, core).
Axes of the slice: x: 4, y: 4, z: 16 (z_hi: 4, z_lo: 4; z = z_hi * 4 + z_lo), core: 2. Of those that a mesh axis runs over, the one named last changes fastest.
Arguments:
- transfer_matrix: float32 [2, 3072, 49152], P(None, 'row', 'mode'), may hold values from -0.01953125 to 0.01953125
- probes: float32 [2, 49152, 256], P(None, ('mode', 'row')), may hold values from -6 to 6
- intensity: float32 [3072, 256], P('row'), may hold values from 0.25 to 4
Outputs:
- gradient: float32 [2, 3072, 49152], P(None, 'row', 'mode')
All inputs are finite; a program needn't handle non-finite values.
Results may differ from a plain program's by a relative error of at most 0.00012.
Values sent between devices are 32-bit elements; how exact they have to be, the bound alone decides.
A program may use at most 64 MiB of HBM per device.

v0:
```python
import jax
import jax.numpy as jnp
from jax import lax
from jax.sharding import Mesh
from jax.sharding import PartitionSpec as P

P_SIZE = 256
ROW = ("row_0", "row_1")
MODE_ROW = ("mode", "row_0", "row_1")


def joined_along(tiles, dim):
    lengths = list(tiles.shape[1:])
    lengths[dim] *= tiles.shape[0]
    return jnp.moveaxis(tiles, 0, dim).reshape(lengths)


def stacked_from(array, axes, turns):
    tiles = array[None]
    for k in turns:
        tiles = lax.all_gather(tiles, axes[k], axis=0, tiled=True)
    block = [lax.axis_size(axes[k]) for k in reversed(turns)]
    tiles = tiles.reshape(*block, *array.shape)
    turned = sorted(range(len(turns)), key=lambda place: turns[len(turns) - 1 - place])
    return tiles.transpose(*turned, *range(len(turns), tiles.ndim)).reshape(-1, *array.shape)


def whole_of(array, axes, turns, dim):
    return joined_along(stacked_from(array, axes, turns), dim)


def split_up(array, dim, count):
    before, after = (array.shape[:dim], array.shape[dim + 1 :])
    return jnp.moveaxis(array.reshape(*before, count, -1, *after), dim, 0)


def sum_at_owner(array, axis, dim):
    count = lax.axis_size(axis)
    tiles = lax.all_to_all(split_up(array, dim, count), axis, 0, 0, tiled=True)
    return jnp.sum(tiles, axis=0)


def sent_to_all(array, axis):
    count = lax.axis_size(axis)
    return lax.all_to_all(
        jnp.broadcast_to(array[None], (count, *array.shape)), axis, 0, 0, tiled=True
    )


def gather_directly(array, axis, dim):
    tiles = sent_to_all(array, axis)
    return joined_along(tiles, dim)


def exact_dot(left, right):
    return jnp.dot(left, right, precision=lax.Precision.HIGHEST, preferred_element_type=jnp.float32)


def exact_dot_transposed(left, right):
    return lax.dot_general(
        left,
        right,
        (((1,), (1,)), ((), ())),
        precision=lax.Precision.HIGHEST,
        preferred_element_type=jnp.float32,
    )


def partial_fields(matrix, strip):
    fields_real = exact_dot(matrix[0], strip[0]) - exact_dot(matrix[1], strip[1])
    fields_imag = exact_dot(matrix[0], strip[1]) + exact_dot(matrix[1], strip[0])
    return jnp.stack([fields_real, fields_imag])


def gradient_columns(residual, strip):
    grad_real = exact_dot_transposed(residual[0], strip[0]) + exact_dot_transposed(
        residual[1], strip[1]
    )
    grad_imag = exact_dot_transposed(residual[1], strip[0]) - exact_dot_transposed(
        residual[0], strip[1]
    )
    return jnp.stack([grad_real, grad_imag])


def make_residual(fields, measured):
    excess = fields[0] * fields[0] + fields[1] * fields[1] - measured
    return excess[None] * fields / P_SIZE


def body(transfer_matrix, probes, intensity):
    strip = whole_of(probes, ROW, (0, 1), 1)
    partial_value = partial_fields(transfer_matrix, strip)
    shares = sum_at_owner(partial_value, "mode", 2)
    share_width = shares.shape[2]
    measured = lax.dynamic_slice_in_dim(
        intensity, lax.axis_index("mode") * share_width, share_width, 1
    )
    residual = gather_directly(make_residual(shares, measured), "mode", 2)
    return gradient_columns(residual, strip)


def solution(mesh):
    split = Mesh(mesh.devices.reshape(4, 4, mesh.shape["mode"]), ("row_0", "row_1", "mode"))
    placed = (P(None, ROW, "mode"), P(None, MODE_ROW, None), P(ROW, None))
    return jax.shard_map(
        body, mesh=split, in_specs=placed, out_specs=P(None, ROW, "mode"), check_vma=False
    )
```

profile of v0, /device:TPU:38, one launch (start us, length us, event | category | flops | bytes accessed | tf_op | source)
XLA Modules:
  0.0 200.2 jit_solution(12416556249650519281)
XLA Ops:
  6.5 0.0 copy-start
  6.5 0.0 all-gather.3.cloned.1.call-start
  6.5 20.1 %all-gather = f32[8,96,256]{2,1,0:T(8,128)} all-gather(f32[2,96,256]{2,1,0:T(8,128)} %param.4), channel_id=2, replica_groups=mesh['row_0'=4,'row_1'=4,'mode'=32] {'row_0'}, dimensions={0}, use_global_device_ids=true | all-gather | bytes 983040 | tf_op jit(solution)/shard_map/all_gather | solution.py:21
  26.6 0.0 all-gather.3.cloned.1.call-update
  26.6 50.7 %all-gather.3.cloned.1.call-done = f32[16,2,96,256]{3,2,1,0:T(8,128)} async-done(((f32[4,2,96,256]{3,2,1,0:T(8,128)}), f32[16,2,96,256]{3,2,1,0:T(8,128)}) %all-gather.3.cloned.1.call-update) | async-done | bytes 3145744 | tf_op jit(solution)/shard_map/all_gather | solution.py:21
  77.4 2.2 %copy.11 = f32[4,4,2,96,256]{4,3,2,1,0:T(8,128)S(1)} copy(f32[4,4,2,96,256]{4,3,2,0,1:T(8,128)} %bitcast.65) | data formatting | bytes 6291456 | tf_op jit(solution)/shard_map/transpose | solution.py:25
  79.6 0.0 copy-start.1
  79.6 0.3 fusion.25
  80.0 1.3 copy-done.1
  81.3 1.2 fusion.4
  82.5 1.2 fusion.2
  83.7 1.9 fusion.10
  85.6 1.8 copy.12
  87.3 3.1 %fusion.13 = f32[192,256]{1,0:T(8,128)} fusion(f32[192,256]{1,0:T(8,128)S(1)} %fusion.2, f32[1536,256]{1,0:T(8,128)S(1)} %bitcast.57, f32[2,192,1536]{2,1,0:T(8,128)} %param.3), kind=kOutput, calls=%fused_computation.14 | convolution fusion | flops 906018816 | bytes 3145728 | tf_op jit(solution)/shard_map/dot_general | solution.py:56
  90.5 1.8 copy.13
  92.2 1.1 maximum_bitcast_fusion
  93.3 0.9 copy.14
  94.1 14.5 %all-to-all-start = ((f32[32,2,192,8]{2,3,1,0:T(8,128)}), f32[32,2,192,8]{2,3,1,0:T(8,128)}, u32[]{:S(2)}, u32[]{:S(2)}) async-start(f32[32,2,192,8]{2,3,1,0:T(8,128)} %copy.14), calls=%async_computation | async-start | bytes 1048576 | tf_op jit(solution)/shard_map/all_to_all | solution.py:39
  108.6 0.0 copy-done
  108.6 0.1 constant_dynamic-slice_fusion
  108.7 0.1 copy.18
  108.8 33.0 %all-to-all-done = f32[32,2,192,8]{2,3,1,0:T(8,128)} async-done(((f32[32,2,192,8]{2,3,1,0:T(8,128)}), f32[32,2,192,8]{2,3,1,0:T(8,128)}, u32[]{:S(2)}, u32[]{:S(2)}) %all-to-all-start) | async-done | bytes 393248 | tf_op jit(solution)/shard_map/all_to_all | solution.py:39
  141.7 1.1 reduce_sum.9
  142.9 0.1 broadcast_in_dim.5
  142.9 38.2 %all_to_all.10 = f32[32,2,192,8]{2,3,1,0:T(8,128)S(1)} all-to-all(f32[32,2,192,8]{2,3,1,0:T(8,128)S(1)} %broadcast_in_dim.5), channel_id=1, replica_groups=mesh['row_0'=4,'row_1'=4,'mode'=32] {'mode'}, dimensions={0} | all-to-all | bytes 786432 | tf_op jit(solution)/shard_map/all_to_all | solution.py:45
  181.1 2.7 %fusion.20 = f32[192,1536]{1,0:T(8,128)S(1)} fusion(f32[1536,256]{1,0:T(8,128)S(1)} %bitcast.54, f32[2,192,32,8]{1,3,0,2:T(8,128)S(1)} %bitcast.61), kind=kOutput, calls=%fused_computation.22 | convolution fusion | flops 905969664 | bytes 3014656 | tf_op jit(solution)/shard_map/dot_general | solution.py:60
  183.8 2.7 %fusion.21 = f32[192,1536]{1,0:T(8,128)S(1)} fusion(f32[1536,256]{1,0:T(8,128)S(1)} %bitcast.55, f32[2,192,32,8]{1,3,0,2:T(8,128)S(1)} %bitcast.62), kind=kOutput, calls=%fused_computation.23 | convolution fusion | flops 905969664 | bytes 3014656 | tf_op jit(solution)/shard_map/dot_general | solution.py:60
  186.5 2.7 %fusion = f32[1,192,1536]{2,1,0:T(8,128)S(1)} fusion(f32[192,1536]{1,0:T(8,128)S(1)} %fusion.20, f32[1536,256]{1,0:T(8,128)S(1)} %bitcast.58, f32[2,192,32,8]{1,3,0,2:T(8,128)S(1)} %bitcast.63), kind=kOutput, calls=%fused_computation.2 | convolution fusion | flops 906264576 | bytes 4194304 | tf_op jit(solution)/shard_map/dot_general | solution.py:60
  189.1 2.7 %fusion.1 = f32[1,192,1536]{2,1,0:T(8,128)S(1)} fusion(f32[192,1536]{1,0:T(8,128)S(1)} %fusion.21, f32[1536,256]{1,0:T(8,128)S(1)} %bitcast.59, f32[2,192,32,8]{1,3,0,2:T(8,128)S(1)} %bitcast.64), kind=kOutput, calls=%fused_computation.3 | convolution fusion | flops 906264576 | bytes 4194304 | tf_op jit(solution)/shard_map/dot_general | solution.py:60
  191.8 1.6 pad_maximum_fusion
  (2 shorter events, 0.0 us)
Async XLA Ops:
  6.5 102.1 %copy-start = (f32[192,256]{1,0:T(8,128)S(1)}, f32[192,256]{1,0:T(8,128)}, u32[]{:S(2)}) copy-start(f32[192,256]{1,0:T(8,128)} %param.5) | copy-start | bytes 589828
  6.5 70.8 %all-gather.3.cloned.1.call-start = ((), (), s32[]{:S(2)}) async-start(), calls=%async_computation.2 | async-start | bytes 3932160 | tf_op jit(solution)/shard_map/all_gather | solution.py:21
  79.6 1.7 copy-start.1
  94.1 47.6 %all-to-all-start = ((f32[32,2,192,8]{2,3,1,0:T(8,128)}), f32[32,2,192,8]{2,3,1,0:T(8,128)}, u32[]{:S(2)}, u32[]{:S(2)}) async-start(f32[32,2,192,8]{2,3,1,0:T(8,128)} %copy.14), calls=%async_computation | async-start | bytes 1048576 | tf_op jit(solution)/shard_map/all_to_all | solution.py:39
Sparse Core Ops, SparseCore 0:
  26.8 50.5 all-gather.2
where the time goes:
time: 201 us; the launch traced here: 200 us
  waiting for transfers between devices  83.7 us (42%)
  blocking collectives  58.3 us (29%)
  matrix products  18.1 us (9%)
  starting transfers between devices  14.5 us (7%)
  between operations  13.5 us (7%)
  local copies, waits for them, and re-layouts  8.45 us (4%)
  other arithmetic  3.73 us (2%)
    all_gather x1, waiting for transfers between devices, stacked_from(): tiles = lax.all_gather(tiles, axes[k], axis=0, tiled=True)  50.7 us
    all_to_all x1, blocking collectives, sent_to_all(): lax.all_to_all(jnp.broadcast_to(array[None], (count, *array.shape)), axis...  38.2 us
    all_to_all x1, waiting for transfers between devices, sum_at_owner(): tiles = lax.all_to_all(split_up(array, dim, count), axis, 0, 0, tiled=True)  33 us
    all_gather x1, blocking collectives, stacked_from(): tiles = lax.all_gather(tiles, axes[k], axis=0, tiled=True)  20.1 us
    all_to_all x1, starting transfers between devices, sum_at_owner(): tiles = lax.all_to_all(split_up(array, dim, count), axis, 0, 0, tiled=True)  14.5 us
    dot_general x4, matrix products, exact_dot_transposed(): lax.dot_general(left, right, (((1,), (1,)), ((), ())), precision=lax.Prec...  10.7 us
    dot_general x4, matrix products, exact_dot(): jnp.dot(left, right, precision=lax.Precision.HIGHEST, preferred_element_t...  7.41 us
  transfers between devices with their start and end apart: 2, of which 2 were waited for; matrix products, arithmetic and copies ran while one was open for 0% of the time, Pallas kernels for 0%

commit v1 on v0

--- a/solution.py
+++ b/solution.py
@@ -18,7 +18,9 @@
 def stacked_from(array, axes, turns):
     tiles = array[None]
     for k in turns:
-        tiles = lax.all_gather(tiles, axes[k], axis=0, tiled=True)
+        tiles = jnp.concatenate(
+            lax.all_to_all(jnp.stack([tiles] * lax.axis_size(axes[k])), axes[k], 0, 0), axis=0
+        )
     block = [lax.axis_size(axes[k]) for k in reversed(turns)]
     tiles = tiles.reshape(*block, *array.shape)
     turned = sorted(range(len(turns)), key=lambda place: turns[len(turns) - 1 - place])

time: 201 us -> 183 us (0.910)
  the two profiles are of different devices: /device:TPU:38 before, /device:TPU:36 now
where the time goes in v1:
time: 183 us; the launch traced here: 182 us
  blocking collectives  104 us (57%)
  waiting for transfers between devices  32.8 us (18%)
  matrix products  18.1 us (10%)
  starting transfers between devices  15.6 us (9%)
  local copies, waits for them, and re-layouts  7.93 us (4%)
  other arithmetic  3.73 us (2%)
    all_to_all x2, blocking collectives, stacked_from(): lax.all_to_all(jnp.stack([tiles] * lax.axis_size(axes[k])), axes[k], 0, 0)  64.5 us
    all_to_all x1, blocking collectives, sent_to_all(): lax.all_to_all(jnp.broadcast_to(array[None], (count, *array.shape)), axis...  39.3 us
    all_to_all x1, waiting for transfers between devices, sum_at_owner(): tiles = lax.all_to_all(split_up(array, dim, count), axis, 0, 0, tiled=True)  32.8 us
    all_to_all x1, starting transfers between devices, sum_at_owner(): tiles = lax.all_to_all(split_up(array, dim, count), axis, 0, 0, tiled=True)  15.6 us
    dot_general x4, matrix products, exact_dot_transposed(): lax.dot_general(left, right, (((1,), (1,)), ((), ())), precision=lax.Prec...  10.7 us
    dot_general x4, matrix products, exact_dot(): jnp.dot(left, right, precision=lax.Precision.HIGHEST, preferred_element_t...  7.44 us
  transfers between devices with their start and end apart: 1, of which 1 were waited for; matrix products, arithmetic and copies ran while one was open for 0% of the time, Pallas kernels for 0%

profile of v1, /device:TPU:36, one launch (start us, length us, event | category | flops | bytes accessed | tf_op | source)
XLA Modules:
  0.0 182.1 jit_solution(3771720269124647582)
XLA Ops:
  0.0 0.0 copy-start
  0.0 1.0 stack.24
  1.0 24.1 %all_to_all.20 = f32[4,1,2,96,256]{4,3,2,1,0:T(8,128)S(1)} all-to-all(f32[4,1,2,96,256]{4,3,2,1,0:T(8,128)S(1)} %stack.24), channel_id=1, replica_groups=mesh['row_0'=4,'row_1'=4,'mode'=32] {'row_0'}, dimensions={0} | all-to-all | bytes 1572864 | tf_op jit(solution)/shard_map/all_to_all | solution.py:22
  25.1 0.4 stack.25
  25.5 40.4 %all_to_all.21 = f32[4,4,2,96,256]{4,3,2,1,0:T(8,128)S(1)} all-to-all(f32[4,4,2,96,256]{4,3,2,1,0:T(8,128)S(1)} %stack.25), channel_id=1, replica_groups=mesh['row_0'=4,'row_1'=4,'mode'=32] {'row_1'}, dimensions={0} | all-to-all | bytes 6291456 | tf_op jit(solution)/shard_map/all_to_all | solution.py:22
  65.9 0.3 copy.7
  66.2 0.0 copy-start.1
  66.2 0.3 fusion.25
  66.6 1.3 copy-done.1
  67.9 1.2 fusion.4
  69.1 1.2 fusion.2
  70.3 1.9 %fusion.10 = f32[192,256]{1,0:T(8,128)} fusion(f32[192,256]{1,0:T(8,128)S(1)} %fusion.4, f32[1536,256]{1,0:T(8,128)S(1)} %bitcast.52, f32[2,192,1536]{2,1,0:T(8,128)S(1)} %copy-done.1), kind=kOutput, calls=%fused_computation.13 | convolution fusion | flops 906018816 | bytes 3145728 | tf_op jit(solution)/shard_map/dot_general | solution.py:58
  72.2 1.7 copy.8
  74.0 3.1 %fusion.13 = f32[192,256]{1,0:T(8,128)} fusion(f32[192,256]{1,0:T(8,128)S(1)} %fusion.2, f32[1536,256]{1,0:T(8,128)S(1)} %bitcast.56, f32[2,192,1536]{2,1,0:T(8,128)} %param.3), kind=kOutput, calls=%fused_computation.14 | convolution fusion | flops 906018816 | bytes 3145728 | tf_op jit(solution)/shard_map/dot_general | solution.py:58
  77.1 1.8 copy.9
  78.9 1.1 maximum_bitcast_fusion
  79.9 0.9 copy.10
  80.8 15.6 %all-to-all-start.2 = ((f32[32,2,192,8]{2,3,1,0:T(8,128)}), f32[32,2,192,8]{2,3,1,0:T(8,128)}, u32[]{:S(2)}, u32[]{:S(2)}) async-start(f32[32,2,192,8]{2,3,1,0:T(8,128)} %copy.10), calls=%async_computation.2 | async-start | bytes 1048576 | tf_op jit(solution)/shard_map/all_to_all | solution.py:41
  96.4 0.0 copy-done
  96.4 0.1 constant_dynamic-slice_fusion
  96.5 0.1 copy.14
  96.5 32.8 %all-to-all-done.2 = f32[32,2,192,8]{2,3,1,0:T(8,128)} async-done(((f32[32,2,192,8]{2,3,1,0:T(8,128)}), f32[32,2,192,8]{2,3,1,0:T(8,128)}, u32[]{:S(2)}, u32[]{:S(2)}) %all-to-all-start.2) | async-done | bytes 393248 | tf_op jit(solution)/shard_map/all_to_all | solution.py:41
  129.3 1.1 reduce_sum.9
  130.4 0.1 broadcast_in_dim.2
  130.5 39.3 %all_to_all.22 = f32[32,2,192,8]{2,3,1,0:T(8,128)S(1)} all-to-all(f32[32,2,192,8]{2,3,1,0:T(8,128)S(1)} %broadcast_in_dim.2), channel_id=1, replica_groups=mesh['row_0'=4,'row_1'=4,'mode'=32] {'mode'}, dimensions={0} | all-to-all | bytes 786432 | tf_op jit(solution)/shard_map/all_to_all | solution.py:47
  169.8 2.7 %fusion.20 = f32[192,1536]{1,0:T(8,128)S(1)} fusion(f32[1536,256]{1,0:T(8,128)S(1)} %bitcast.53, f32[2,192,32,8]{1,3,0,2:T(8,128)S(1)} %bitcast.60), kind=kOutput, calls=%fused_computation.22 | convolution fusion | flops 905969664 | bytes 3014656 | tf_op jit(solution)/shard_map/dot_general | solution.py:62
  172.5 2.7 %fusion.21 = f32[192,1536]{1,0:T(8,128)S(1)} fusion(f32[1536,256]{1,0:T(8,128)S(1)} %bitcast.54, f32[2,192,32,8]{1,3,0,2:T(8,128)S(1)} %bitcast.61), kind=kOutput, calls=%fused_computation.23 | convolution fusion | flops 905969664 | bytes 3014656 | tf_op jit(solution)/shard_map/dot_general | solution.py:62
  175.1 2.7 %fusion = f32[1,192,1536]{2,1,0:T(8,128)S(1)} fusion(f32[192,1536]{1,0:T(8,128)S(1)} %fusion.20, f32[1536,256]{1,0:T(8,128)S(1)} %bitcast.57, f32[2,192,32,8]{1,3,0,2:T(8,128)S(1)} %bitcast.62), kind=kOutput, calls=%fused_computation.2 | convolution fusion | flops 906264576 | bytes 4194304 | tf_op jit(solution)/shard_map/dot_general | solution.py:62
  177.8 2.7 %fusion.1 = f32[1,192,1536]{2,1,0:T(8,128)S(1)} fusion(f32[192,1536]{1,0:T(8,128)S(1)} %fusion.21, f32[1536,256]{1,0:T(8,128)S(1)} %bitcast.58, f32[2,192,32,8]{1,3,0,2:T(8,128)S(1)} %bitcast.63), kind=kOutput, calls=%fused_computation.3 | convolution fusion | flops 906264576 | bytes 4194304 | tf_op jit(solution)/shard_map/dot_general | solution.py:62
  180.5 1.6 pad_maximum_fusion
  (2 shorter events, 0.0 us)
Async XLA Ops:
  0.0 96.4 %copy-start = (f32[192,256]{1,0:T(8,128)S(1)}, f32[192,256]{1,0:T(8,128)}, u32[]{:S(2)}) copy-start(f32[192,256]{1,0:T(8,128)} %param.5) | copy-start | bytes 589828
  66.2 1.7 copy-start.1
  80.8 48.5 %all-to-all-start.2 = ((f32[32,2,192,8]{2,3,1,0:T(8,128)}), f32[32,2,192,8]{2,3,1,0:T(8,128)}, u32[]{:S(2)}, u32[]{:S(2)}) async-start(f32[32,2,192,8]{2,3,1,0:T(8,128)} %copy.10), calls=%async_computation.2 | async-start | bytes 1048576 | tf_op jit(solution)/shard_map/all_to_all | solution.py:41
